TPU v7x, 256 devices: a whole 4x4x8 slice. The times are simulated.
256 devices in a mesh: section: 8 (over z), dp: 32 (over x, y, core).
Axes of the slice: x: 4, y: 4, z: 8, core: 2. Of those that a mesh axis runs over, the one named last changes fastest.
Arguments:
- inputs: bfloat16 [8192, 2048], P('dp'), may hold values from -6 to 6
- order: int32 [32, 2], P('dp'), may hold values from 0 to 1, each once within a row
- image_start: int32 [32, 2], P('dp'), may hold values from 0 to 112, as said below
- image_len: int32 [32, 2], P('dp'), may hold values from 16 to 64
- norm_gain: float32 [8, 2048], P('section'), may hold values from 0.25 to 1.75
- qkv_weight: bfloat16 [8, 2048, 6144], P('section', 'dp'), may hold values from -0.125 to 0.125
- q_gain: float32 [8, 2048], P('section'), may hold values from 0.5 to 2.5
- k_gain: float32 [8, 2048], P('section'), may hold values from 0.5 to 2.5
- o_weight: bfloat16 [8, 2048, 2048], P('section'), may hold values from -0.125 to 0.125
Outputs:
- section_outputs: bfloat16 [8, 8192, 2048], P('section', 'dp')
Inputs may be any that keep to these rules, and one draw needn't show every extreme that they name: `order`: each row is a permutation of the micro-batch numbers. image_start + image_len <= 128 for every micro-batch.
All inputs are finite; a program needn't handle non-finite values.
Results may differ from a plain program's by a relative error of at most 0.035.
Values may be sent and summed in bfloat16 or wider, within the bound.
No kernel may reach another device: no remote copies, remote signals or barrier semaphores. Data moves between devices by JAX's collectives and lax.ppermute only.
A program may use at most 128 MiB of HBM per device.

v0:
```python
import jax
import jax.numpy as jnp
from jax import lax
from jax.sharding import PartitionSpec as P

HEADS = 16
HEAD_DIM = 128


epsilon_value = 1e-05


def from_behind(shard, axis, by):
    devices = lax.axis_size(axis)
    pairs = [(i, i + by) for i in range(devices) if 0 <= i + by < devices]
    return lax.ppermute(shard, axis, pairs)


def normalize(hidden, gain):
    widened = hidden.astype(jnp.float32)
    mean_square = jnp.mean(widened * widened, axis=-1, keepdims=True)
    return (widened * lax.rsqrt(mean_square + epsilon_value) * gain).astype(jnp.bfloat16)


def head_norm(block, gain, seq_len):
    split = block.reshape(seq_len, HEADS, HEAD_DIM)
    mean_square = jnp.mean(split * split, axis=-1, keepdims=True)
    return (split * lax.rsqrt(mean_square + epsilon_value) * gain.reshape(HEADS, HEAD_DIM)).astype(
        jnp.bfloat16
    )


def finish(hidden, projected, gain_query, gain_key, out_weight, start, length):
    seq_len, model_width = hidden.shape
    queries = head_norm(projected[:, :model_width], gain_query, seq_len)
    key_rows = head_norm(projected[:, model_width : 2 * model_width], gain_key, seq_len)
    value_rows = (
        projected[:, 2 * model_width :].astype(jnp.bfloat16).reshape(seq_len, HEADS, HEAD_DIM)
    )
    scores = jnp.einsum(
        "qhd,khd->hqk", queries, key_rows, preferred_element_type=jnp.float32
    ) * HEAD_DIM ** (-0.5)
    position = jnp.arange(seq_len, dtype=jnp.int32)
    in_image = (position >= start) & (position < start + length)
    allowed = (position[None, :] <= position[:, None]) | in_image[:, None] & in_image[None, :]
    scores = jnp.where(allowed[None], scores, -1e30)
    row_max = jnp.max(scores, axis=-1, keepdims=True)
    lifted = jnp.exp(scores - row_max)
    probabilities = (lifted / jnp.sum(lifted, axis=-1, keepdims=True)).astype(jnp.bfloat16)
    mixed = jnp.einsum(
        "hqk,khd->qhd", probabilities, value_rows, preferred_element_type=jnp.float32
    )
    attended = mixed.reshape(seq_len, model_width).astype(jnp.bfloat16)
    output_rows = jnp.dot(attended, out_weight, preferred_element_type=jnp.float32)
    return (hidden.astype(jnp.float32) + output_rows).astype(jnp.bfloat16)


def body(inputs, order, image_start, image_len, norm_gain, qkv_weight, q_gain, k_gain, o_weight):
    section_count = lax.axis_size("section")
    section_index = lax.axis_index("section")
    micro_count = order.shape[1]
    row_count, model_width = inputs.shape
    seq_len = row_count // micro_count
    ordered = jnp.take(inputs.reshape(micro_count, seq_len, model_width), order[0], axis=0)
    starts = jnp.take(image_start[0], order[0])
    lengths = jnp.take(image_len[0], order[0])
    gain = norm_gain[0]
    gain_query = q_gain[0]
    gain_key = k_gain[0]
    out_weight = o_weight[0]
    shard = qkv_weight[0]
    turns = micro_count + section_count - 1

    def entering(turn_index, incoming):
        fresh = lax.dynamic_index_in_dim(
            ordered, jnp.clip(turn_index, 0, micro_count - 1), 0, keepdims=False
        )
        return jnp.where(section_index == 0, fresh, incoming)

    def settle(turn_index, hidden, project_rows, outputs):
        slot_index = turn_index - section_index
        active = (slot_index >= 0) & (slot_index < micro_count)
        chosen = jnp.clip(slot_index, 0, micro_count - 1)

        def compute(state):
            return finish(
                state,
                project_rows(state),
                gain_query,
                gain_key,
                out_weight,
                starts[chosen],
                lengths[chosen],
            )

        result = lax.cond(active, compute, lambda state: state, hidden)
        outputs = jnp.where(
            active, lax.dynamic_update_index_in_dim(outputs, result, chosen, 0), outputs
        )
        incoming = from_behind(result, "section", 1)
        return (incoming, outputs)

    outputs = jnp.zeros((micro_count, seq_len, model_width), jnp.bfloat16)
    incoming = jnp.zeros((seq_len, model_width), jnp.bfloat16)
    gathered = lax.all_gather(shard, "dp", axis=0, tiled=True)
    first_turn = 0

    def project(state):
        return jnp.dot(normalize(state, gain), gathered, preferred_element_type=jnp.float32)

    def advance(turn_index, carry):
        arriving, collected = carry
        hidden_now = entering(turn_index, arriving)
        return settle(turn_index, hidden_now, project, collected)

    incoming, outputs = lax.fori_loop(first_turn, turns, advance, (incoming, outputs))
    return outputs.reshape(1, row_count, model_width)


def solution(mesh):
    in_specs = (
        P("dp", None),
        P("dp", None),
        P("dp", None),
        P("dp", None),
        P("section", None),
        P("section", "dp", None),
        P("section", None),
        P("section", None),
        P("section", None, None),
    )
    out_specs = P("section", "dp", None)
    return jax.shard_map(body, mesh=mesh, in_specs=in_specs, out_specs=out_specs, check_vma=False)
```

profile of v0, /device:TPU:224, one launch (start us, length us, event | category | flops | bytes accessed | tf_op | source)
XLA Modules:
  0.0 543.5 jit_solution(1400201827899361241)
XLA Ops:
  7.9 1.3 gather_fusion.2
  9.2 1.3 gather_fusion.1
  12.5 1.1 broadcast_select_fusion
  13.6 93.9 %all-gather.3.cloned.1.call-done = bf16[1,2048,6144]{2,1,0:T(8,128)(2,1)} async-done(((bf16[1,64,6144]{2,1,0:T(8,128)(2,1)}), bf16[1,2048,6144]{2,1,0:T(8,128)(2,1)}) %all-gather.3.cloned.1.call-update) | async-done | bytes 25165840 | tf_op jit(solution)/shard_map/all_gather | solution.py:105
  107.6 1.1 broadcast_in_dim.57
  108.6 428.0 %while.16 = (s32[]{:T(128)}, bf16[128,2048]{1,0:T(8,128)(2,1)S(1)}, bf16[2,128,2048]{2,1,0:T(8,128)(2,1)}, s32[]{:T(128)}, pred[]{:T(512)}, /*index=5*/bf16[2,12...) while((s32[]{:T(128)}, bf16[128,2048]{1,0:T(8,128)(2,1)S(1)}, ...), condition=%wide.region_8.10_spmd, body=%wide.region_0.9_spmd.sunk | while | flops 4437105152 | bytes 82586920 | solution.py:116
  108.6 1.1 bitcast_select_fusion.3
  109.8 1.3 collective-permute-start
  111.1 2.0 fusion.27
  113.0 12.7 %collective-permute-done = bf16[128,2048]{1,0:T(8,128)(2,1)S(1)} collective-permute-done((bf16[128,2048]{1,0:T(8,128)(2,1)S(1)}, bf16[128,2048]{1,0:T(8,128)(2,1)S(1)}, u32[]{:S(2)}, u32[]{:S(2)}) %collective-permute-start) | collective-permute-done | bytes 524320 | tf_op jit(solution)/shard_map/while/body/eval_jaxpr/ppermute | solution.py:16
  125.7 1.1 bitcast_select_fusion.3
  126.9 1.3 collective-permute-start
  128.2 2.0 fusion.27
  130.1 11.9 %collective-permute-done = bf16[128,2048]{1,0:T(8,128)(2,1)S(1)} collective-permute-done((bf16[128,2048]{1,0:T(8,128)(2,1)S(1)}, bf16[128,2048]{1,0:T(8,128)(2,1)S(1)}, u32[]{:S(2)}, u32[]{:S(2)}) %collective-permute-start) | collective-permute-done | bytes 524320 | tf_op jit(solution)/shard_map/while/body/eval_jaxpr/ppermute | solution.py:16
  142.0 1.1 bitcast_select_fusion.3
  143.2 1.3 collective-permute-start
  144.5 2.0 fusion.27
  146.4 11.0 %collective-permute-done = bf16[128,2048]{1,0:T(8,128)(2,1)S(1)} collective-permute-done((bf16[128,2048]{1,0:T(8,128)(2,1)S(1)}, bf16[128,2048]{1,0:T(8,128)(2,1)S(1)}, u32[]{:S(2)}, u32[]{:S(2)}) %collective-permute-start) | collective-permute-done | bytes 524320 | tf_op jit(solution)/shard_map/while/body/eval_jaxpr/ppermute | solution.py:16
  157.4 1.1 bitcast_select_fusion.3
  158.5 1.3 collective-permute-start
  159.8 2.0 fusion.27
  161.8 11.1 %collective-permute-done = bf16[128,2048]{1,0:T(8,128)(2,1)S(1)} collective-permute-done((bf16[128,2048]{1,0:T(8,128)(2,1)S(1)}, bf16[128,2048]{1,0:T(8,128)(2,1)S(1)}, u32[]{:S(2)}, u32[]{:S(2)}) %collective-permute-start) | collective-permute-done | bytes 524320 | tf_op jit(solution)/shard_map/while/body/eval_jaxpr/ppermute | solution.py:16
  172.9 1.1 bitcast_select_fusion.3
  174.0 1.3 collective-permute-start
  175.3 2.0 fusion.27
  177.3 10.3 %collective-permute-done = bf16[128,2048]{1,0:T(8,128)(2,1)S(1)} collective-permute-done((bf16[128,2048]{1,0:T(8,128)(2,1)S(1)}, bf16[128,2048]{1,0:T(8,128)(2,1)S(1)}, u32[]{:S(2)}, u32[]{:S(2)}) %collective-permute-start) | collective-permute-done | bytes 524320 | tf_op jit(solution)/shard_map/while/body/eval_jaxpr/ppermute | solution.py:16
  187.5 1.1 bitcast_select_fusion.3
  188.7 1.3 collective-permute-start
  190.0 2.0 fusion.27
  191.9 9.4 %collective-permute-done = bf16[128,2048]{1,0:T(8,128)(2,1)S(1)} collective-permute-done((bf16[128,2048]{1,0:T(8,128)(2,1)S(1)}, bf16[128,2048]{1,0:T(8,128)(2,1)S(1)}, u32[]{:S(2)}, u32[]{:S(2)}) %collective-permute-start) | collective-permute-done | bytes 524320 | tf_op jit(solution)/shard_map/while/body/eval_jaxpr/ppermute | solution.py:16
  201.3 1.1 bitcast_select_fusion.3
  202.5 1.3 collective-permute-start
  203.8 2.0 fusion.27
  205.7 238.5 %collective-permute-done = bf16[128,2048]{1,0:T(8,128)(2,1)S(1)} collective-permute-done((bf16[128,2048]{1,0:T(8,128)(2,1)S(1)}, bf16[128,2048]{1,0:T(8,128)(2,1)S(1)}, u32[]{:S(2)}, u32[]{:S(2)}) %collective-permute-start) | collective-permute-done | bytes 524320 | tf_op jit(solution)/shard_map/while/body/eval_jaxpr/ppermute | solution.py:16
  444.2 1.1 bitcast_select_fusion.3
  445.3 33.6 %conditional.2 = (bf16[128,2048]{1,0:T(8,128)(2,1)S(1)}) conditional(s32[]{:T(128)} %convert_element_type.56, bf16[128,2048]{1,0:T(8,128)(2,1)S(1)} %bitcast_select_fusion.3, (bf16[128,2048]{1,0:T(8,128)(2,1)S(1)}, f32[1,2048]{1,0:T(1,128)}, bf16[2048,6144]{1,0:T(8,128)(2,1)}, s32[]{:T(128)}, s32[2]{0:T(128)S(1)}, /*index=5*/s32[2]{0:T(128)S(1)}, ...), branch_computations={%region_1.2_spmd, %region_2.8_spmd} | conditional | flops 4436580864 | bytes 77343176 | solution.py:96
  445.5 10.1 %fusion.8 = f32[128,6144]{1,0:T(8,128)S(1)} fusion(bf16[2048,6144]{1,0:T(8,128)(2,1)} %get-tuple-element.278, bf16[128,2048]{1,0:T(8,128)(2,1)S(1)} %get-tuple-element.276, f32[2048]{0:T(1024)} %bitcast.57, f32[128]{0:T(128)S(1)} %add_rsqrt_fusion.2), kind=kOutput, calls=%fused_computation.24 | convolution fusion | flops 3222274048 | bytes 28844544 | tf_op jit(solution)/shard_map/while/body/eval_jaxpr/cond/branch_1_fun/dot_general | solution.py:109
  455.7 1.7 copy-done.1
  457.5 1.0 copy.31
  458.5 2.8 slice_bitcast_fusion.1
  462.0 1.4 copy.32
  463.4 1.1 copy-done.2
  465.0 2.7 multiply_convert_fusion
  470.8 1.7 fusion.4
  472.7 1.5 convolution_convert_fusion
  474.2 4.7 fusion.1
  478.9 1.3 collective-permute-start
  480.2 2.0 fusion.27
  482.1 8.8 %collective-permute-done = bf16[128,2048]{1,0:T(8,128)(2,1)S(1)} collective-permute-done((bf16[128,2048]{1,0:T(8,128)(2,1)S(1)}, bf16[128,2048]{1,0:T(8,128)(2,1)S(1)}, u32[]{:S(2)}, u32[]{:S(2)}) %collective-permute-start) | collective-permute-done | bytes 524320 | tf_op jit(solution)/shard_map/while/body/eval_jaxpr/ppermute | solution.py:16
  491.0 1.1 bitcast_select_fusion.3
  492.1 33.6 %conditional.2 = (bf16[128,2048]{1,0:T(8,128)(2,1)S(1)}) conditional(s32[]{:T(128)} %convert_element_type.56, bf16[128,2048]{1,0:T(8,128)(2,1)S(1)} %bitcast_select_fusion.3, (bf16[128,2048]{1,0:T(8,128)(2,1)S(1)}, f32[1,2048]{1,0:T(1,128)}, bf16[2048,6144]{1,0:T(8,128)(2,1)}, s32[]{:T(128)}, s32[2]{0:T(128)S(1)}, /*index=5*/s32[2]{0:T(128)S(1)}, ...), branch_computations={%region_1.2_spmd, %region_2.8_spmd} | conditional | flops 4436580864 | bytes 77343176 | solution.py:96
  492.3 10.1 %fusion.8 = f32[128,6144]{1,0:T(8,128)S(1)} fusion(bf16[2048,6144]{1,0:T(8,128)(2,1)} %get-tuple-element.278, bf16[128,2048]{1,0:T(8,128)(2,1)S(1)} %get-tuple-element.276, f32[2048]{0:T(1024)} %bitcast.57, f32[128]{0:T(128)S(1)} %add_rsqrt_fusion.2), kind=kOutput, calls=%fused_computation.24 | convolution fusion | flops 3222274048 | bytes 28844544 | tf_op jit(solution)/shard_map/while/body/eval_jaxpr/cond/branch_1_fun/dot_general | solution.py:109
  502.4 1.7 copy-done.1
  504.2 1.0 copy.31
  505.2 2.8 slice_bitcast_fusion.1
  508.7 1.4 copy.32
  510.1 1.1 copy-done.2
  511.8 2.7 multiply_convert_fusion
  517.5 1.7 fusion.4
  519.4 1.5 convolution_convert_fusion
  520.9 4.7 fusion.1
  525.6 1.3 collective-permute-start
  526.9 2.0 fusion.27
  528.9 7.8 %collective-permute-done = bf16[128,2048]{1,0:T(8,128)(2,1)S(1)} collective-permute-done((bf16[128,2048]{1,0:T(8,128)(2,1)S(1)}, bf16[128,2048]{1,0:T(8,128)(2,1)S(1)}, u32[]{:S(2)}, u32[]{:S(2)}) %collective-permute-start) | collective-permute-done | bytes 524320 | tf_op jit(solution)/shard_map/while/body/eval_jaxpr/ppermute | solution.py:16
  (65 shorter events, 10.6 us)
Async XLA Ops:
  6.5 4.7 copy-start
  6.5 101.0 %all-gather.3.cloned.1.call-start = ((), (), s32[]{:S(2)}) async-start(), calls=%async_computation | async-start | bytes 25952256 | tf_op jit(solution)/shard_map/all_gather | solution.py:105
  109.8 16.0 %collective-permute-start = (bf16[128,2048]{1,0:T(8,128)(2,1)S(1)}, bf16[128,2048]{1,0:T(8,128)(2,1)S(1)}, u32[]{:S(2)}, u32[]{:S(2)}) collective-permute-start(bf16[128,2048]{1,0:T(8,128)(2,1)S(1)} %get-tuple-element.460), channel_id=1, source_target_pairs={{0,32},{32,64},{64,96},{96,128},{128,160},{160,192},{192,224},{1,3... | collective-permute-start | bytes 1572872 | tf_op jit(solution)/shard_map/while/body/eval_jaxpr/ppermute | solution.py:16
  126.9 15.2 %collective-permute-start = (bf16[128,2048]{1,0:T(8,128)(2,1)S(1)}, bf16[128,2048]{1,0:T(8,128)(2,1)S(1)}, u32[]{:S(2)}, u32[]{:S(2)}) collective-permute-start(bf16[128,2048]{1,0:T(8,128)(2,1)S(1)} %get-tuple-element.460), channel_id=1, source_target_pairs={{0,32},{32,64},{64,96},{96,128},{128,160},{160,192},{192,224},{1,3... | collective-permute-start | bytes 1572872 | tf_op jit(solution)/shard_map/while/body/eval_jaxpr/ppermute | solution.py:16
  143.2 14.2 %collective-permute-start = (bf16[128,2048]{1,0:T(8,128)(2,1)S(1)}, bf16[128,2048]{1,0:T(8,128)(2,1)S(1)}, u32[]{:S(2)}, u32[]{:S(2)}) collective-permute-start(bf16[128,2048]{1,0:T(8,128)(2,1)S(1)} %get-tuple-element.460), channel_id=1, source_target_pairs={{0,32},{32,64},{64,96},{96,128},{128,160},{160,192},{192,224},{1,3... | collective-permute-start | bytes 1572872 | tf_op jit(solution)/shard_map/while/body/eval_jaxpr/ppermute | solution.py:16
  158.5 14.4 %collective-permute-start = (bf16[128,2048]{1,0:T(8,128)(2,1)S(1)}, bf16[128,2048]{1,0:T(8,128)(2,1)S(1)}, u32[]{:S(2)}, u32[]{:S(2)}) collective-permute-start(bf16[128,2048]{1,0:T(8,128)(2,1)S(1)} %get-tuple-element.460), channel_id=1, source_target_pairs={{0,32},{32,64},{64,96},{96,128},{128,160},{160,192},{192,224},{1,3... | collective-permute-start | bytes 1572872 | tf_op jit(solution)/shard_map/while/body/eval_jaxpr/ppermute | solution.py:16
  174.0 13.5 %collective-permute-start = (bf16[128,2048]{1,0:T(8,128)(2,1)S(1)}, bf16[128,2048]{1,0:T(8,128)(2,1)S(1)}, u32[]{:S(2)}, u32[]{:S(2)}) collective-permute-start(bf16[128,2048]{1,0:T(8,128)(2,1)S(1)} %get-tuple-element.460), channel_id=1, source_target_pairs={{0,32},{32,64},{64,96},{96,128},{128,160},{160,192},{192,224},{1,3... | collective-permute-start | bytes 1572872 | tf_op jit(solution)/shard_map/while/body/eval_jaxpr/ppermute | solution.py:16
  188.7 12.7 %collective-permute-start = (bf16[128,2048]{1,0:T(8,128)(2,1)S(1)}, bf16[128,2048]{1,0:T(8,128)(2,1)S(1)}, u32[]{:S(2)}, u32[]{:S(2)}) collective-permute-start(bf16[128,2048]{1,0:T(8,128)(2,1)S(1)} %get-tuple-element.460), channel_id=1, source_target_pairs={{0,32},{32,64},{64,96},{96,128},{128,160},{160,192},{192,224},{1,3... | collective-permute-start | bytes 1572872 | tf_op jit(solution)/shard_map/while/body/eval_jaxpr/ppermute | solution.py:16
  202.5 241.7 %collective-permute-start = (bf16[128,2048]{1,0:T(8,128)(2,1)S(1)}, bf16[128,2048]{1,0:T(8,128)(2,1)S(1)}, u32[]{:S(2)}, u32[]{:S(2)}) collective-permute-start(bf16[128,2048]{1,0:T(8,128)(2,1)S(1)} %get-tuple-element.460), channel_id=1, source_target_pairs={{0,32},{32,64},{64,96},{96,128},{128,160},{160,192},{192,224},{1,3... | collective-permute-start | bytes 1572872 | tf_op jit(solution)/shard_map/while/body/eval_jaxpr/ppermute | solution.py:16
  455.6 1.8 copy-start.1
  457.4 7.6 %copy-start.3 = (f32[1,2048]{1,0:T(1,128)S(1)}, f32[1,2048]{1,0:T(1,128)}, u32[]{:S(2)}) copy-start(f32[1,2048]{1,0:T(1,128)} %get-tuple-element.282) | copy-start | bytes 24580 | tf_op jit(solution)/shard_map/while/body/eval_jaxpr/cond
  457.4 7.6 %copy-start.4 = (f32[1,2048]{1,0:T(1,128)S(1)}, f32[1,2048]{1,0:T(1,128)}, u32[]{:S(2)}) copy-start(f32[1,2048]{1,0:T(1,128)} %get-tuple-element.283) | copy-start | bytes 24580 | tf_op jit(solution)/shard_map/while/body/eval_jaxpr/cond
  463.4 1.1 copy-start.2
  478.9 12.1 %collective-permute-start = (bf16[128,2048]{1,0:T(8,128)(2,1)S(1)}, bf16[128,2048]{1,0:T(8,128)(2,1)S(1)}, u32[]{:S(2)}, u32[]{:S(2)}) collective-permute-start(bf16[128,2048]{1,0:T(8,128)(2,1)S(1)} %get-tuple-element.460), channel_id=1, source_target_pairs={{0,32},{32,64},{64,96},{96,128},{128,160},{160,192},{192,224},{1,3... | collective-permute-start | bytes 1572872 | tf_op jit(solution)/shard_map/while/body/eval_jaxpr/ppermute | solution.py:16
  502.4 1.8 copy-start.1
  504.2 7.6 %copy-start.3 = (f32[1,2048]{1,0:T(1,128)S(1)}, f32[1,2048]{1,0:T(1,128)}, u32[]{:S(2)}) copy-start(f32[1,2048]{1,0:T(1,128)} %get-tuple-element.282) | copy-start | bytes 24580 | tf_op jit(solution)/shard_map/while/body/eval_jaxpr/cond
  504.2 7.6 %copy-start.4 = (f32[1,2048]{1,0:T(1,128)S(1)}, f32[1,2048]{1,0:T(1,128)}, u32[]{:S(2)}) copy-start(f32[1,2048]{1,0:T(1,128)} %get-tuple-element.283) | copy-start | bytes 24580 | tf_op jit(solution)/shard_map/while/body/eval_jaxpr/cond
  510.1 1.1 copy-start.2
  525.6 11.1 %collective-permute-start = (bf16[128,2048]{1,0:T(8,128)(2,1)S(1)}, bf16[128,2048]{1,0:T(8,128)(2,1)S(1)}, u32[]{:S(2)}, u32[]{:S(2)}) collective-permute-start(bf16[128,2048]{1,0:T(8,128)(2,1)S(1)} %get-tuple-element.460), channel_id=1, source_target_pairs={{0,32},{32,64},{64,96},{96,128},{128,160},{160,192},{192,224},{1,3... | collective-permute-start | bytes 1572872 | tf_op jit(solution)/shard_map/while/body/eval_jaxpr/ppermute | solution.py:16
Sparse Core Ops, SparseCore 0:
  9.9 97.5 all-gather.2
where the time goes:
time: 545 us; the launch traced here: 544 us
  waiting for transfers between devices  416 us (76%)
  other arithmetic  39.8 us (7%)
  matrix products  35.9 us (7%)
  local copies, waits for them, and re-layouts  23.8 us (4%)
  between operations  13.4 us (2%)
  starting transfers between devices  11.6 us (2%)
    ppermute x9, waiting for transfers between devices, from_behind(): return lax.ppermute(shard, axis, pairs)  321 us
    all_gather x1, waiting for transfers between devices, body(): gathered = lax.all_gather(shard, 'dp', axis=0, tiled=True)  93.9 us
    dot_general x2, matrix products, project(): jnp.dot(normalize(state, gain), gathered, preferred_element_type=jnp.floa...  20.3 us
    select_n x9, other arithmetic, settle(): jnp.where(active, lax.dynamic_update_index_in_dim(outputs, result, chosen...  17.7 us
    cond x22, local copies, waits for them, and re-layouts  14.4 us
    ppermute x9, starting transfers between devices, from_behind(): return lax.ppermute(shard, axis, pairs)  11.6 us
  transfers between devices with their start and end apart: 10, of which 10 were waited for; matrix products, arithmetic and copies ran while one was open for 4% of the time, Pallas kernels for 0%

commit v1 on v0

v1 whole, which is shorter than its diff:
```python
import functools
import math

import jax
import jax.numpy as jnp
from jax import lax
from jax.experimental import pallas as pl
from jax.experimental.pallas import tpu as pltpu
from jax.sharding import PartitionSpec as P

HEADS = 16
HEAD_DIM = 128
GROUPS = 4
RESIDENT = 2
EPSILON = 1e-05
MIB = 1 << 20

ANY = pl.BlockSpec(memory_space=pl.ANY)
VMEM = pl.BlockSpec(memory_space=pltpu.VMEM)


def group_copies(w_hbm, target_of, sem_of, groups, width):
    model = w_hbm.shape[0]
    span = width // GROUPS
    copies = []
    for place, group in enumerate(groups):
        target = target_of(place)
        for part in range(3):
            copies.append(
                pltpu.make_async_copy(
                    w_hbm.at[:, pl.ds(part * width + group * span, span)],
                    target.at[:, pl.ds(part * span, span)],
                    sem_of(place, part),
                )
            )
    return copies


def load_body(w_hbm, o_hbm, w_keep, o_keep, w_sem, o_sem):
    model = o_hbm.shape[0]
    copies = group_copies(
        w_hbm, lambda place: w_keep.at[place], lambda place, part: w_sem.at[place, part],
        range(RESIDENT), model,
    )
    copies.append(pltpu.make_async_copy(o_hbm, o_keep, o_sem))
    for copy in copies:
        copy.start()
    for copy in copies:
        copy.wait()


def load_weights(qkv, out_weight):
    model = out_weight.shape[0]
    return pl.pallas_call(
        load_body,
        out_shape=(
            pltpu.VMEM((RESIDENT, model, 3 * model // GROUPS), qkv.dtype),
            pltpu.VMEM(out_weight.shape, out_weight.dtype),
        ),
        in_specs=[ANY, ANY],
        out_specs=[VMEM, VMEM],
        scratch_shapes=[pltpu.SemaphoreType.DMA((RESIDENT, 3)), pltpu.SemaphoreType.DMA],
        compiler_params=pltpu.CompilerParams(vmem_limit_bytes=1 * MIB),
        name="load_weights",
    )(qkv, out_weight)


def head_scale(block, ones):
    square = (block * block).astype(jnp.bfloat16)
    parts = []
    for at in range(0, block.shape[1], 2 * HEAD_DIM):
        parts.append(
            jnp.dot(
                square[:, at : at + 2 * HEAD_DIM], ones, preferred_element_type=jnp.float32
            )
        )
    total = jnp.concatenate(parts, axis=1)
    return lax.rsqrt(total * (1.0 / HEAD_DIM) + EPSILON)


def attend(projected, gain_query, gain_key, allowed, ones_pair, ones_column, span):
    query = projected[:, :span]
    key = projected[:, span : 2 * span]
    value = projected[:, 2 * span :].astype(jnp.bfloat16)
    query = (query * head_scale(query, ones_pair) * gain_query).astype(jnp.bfloat16)
    key = (key * head_scale(key, ones_pair) * gain_key).astype(jnp.bfloat16)
    heads = []
    for at in range(0, span, HEAD_DIM):
        cut = slice(at, at + HEAD_DIM)
        scores = lax.dot_general(
            query[:, cut], key[:, cut], (((1,), (1,)), ((), ())), preferred_element_type=jnp.float32
        )
        lifted = (jnp.exp2(scores) * allowed).astype(jnp.bfloat16)
        spread = jnp.concatenate([value[:, cut], ones_column], axis=1)
        mixed = jnp.dot(lifted, spread, preferred_element_type=jnp.float32)
        heads.append((mixed[:, :HEAD_DIM] / mixed[:, HEAD_DIM:]).astype(jnp.bfloat16))
    return heads


def turn_body(turn, last, micro, *refs):
    refs = list(refs)
    fresh_ref = refs.pop(0) if turn < micro else None
    hidden_ref = refs.pop(0) if turn > 0 else None
    before_ref = refs.pop(0) if turn > 0 else None
    if turn > 1:
        refs.pop(0)
    (allowed_ref, gain_ref, gain_query_ref, gain_key_ref, ones_ref, keep_ref, w_hbm, o_ref) = refs[:8]
    refs = refs[8:]
    after_ref = None if last else refs.pop(0)
    outputs = refs.pop(0) if turn > 0 else None
    state, normed, attended, stream, final, stream_sem, write_sem, final_sem = refs

    model = o_ref.shape[0]
    span = model // GROUPS
    section = lax.axis_index("section")
    slot = turn - section
    active = (slot >= 0) & (slot < micro)
    wrote = (slot >= 1) & (slot <= micro)

    if turn > 0:
        earlier = pltpu.make_async_copy(
            before_ref, outputs.at[jnp.clip(slot - 1, 0, micro - 1)], write_sem
        )

        @pl.when(wrote)
        def _():
            earlier.start()

    @pl.when(active)
    def _():
        streamed = group_copies(
            w_hbm, lambda place: stream.at[place], lambda place, part: stream_sem.at[place, part],
            range(RESIDENT, GROUPS), model,
        )
        for copy in streamed:
            copy.start()
        if turn == 0:
            state[...] = fresh_ref[0]
        elif turn < micro:

            @pl.when(section == 0)
            def _():
                state[...] = fresh_ref[turn]

            @pl.when(section != 0)
            def _():
                state[...] = hidden_ref[...]

        else:
            state[...] = hidden_ref[...]
        widened = state[...].astype(jnp.float32)
        mean_square = jnp.mean(widened * widened, axis=-1, keepdims=True)
        normed[...] = (widened * lax.rsqrt(mean_square + EPSILON) * gain_ref[...]).astype(
            jnp.bfloat16
        )
        allowed = allowed_ref[jnp.clip(slot, 0, micro - 1)]
        ones_pair = ones_ref[...]
        ones_column = jnp.ones((state.shape[0], HEAD_DIM), jnp.bfloat16)

        def project(group):
            if group < RESIDENT:
                weight = keep_ref.at[group]
            else:
                for copy in streamed[3 * (group - RESIDENT) : 3 * (group - RESIDENT) + 3]:
                    copy.wait()
                weight = stream.at[group - RESIDENT]
            return jnp.dot(normed[...], weight[...], preferred_element_type=jnp.float32)

        projected = project(0)
        for group in range(GROUPS):
            following = project(group + 1) if group + 1 < GROUPS else None
            cut = slice(group * span, (group + 1) * span)
            heads = attend(
                projected, gain_query_ref[:, cut], gain_key_ref[:, cut], allowed, ones_pair,
                ones_column, span,
            )
            for at, head in enumerate(heads):
                attended[:, group * span + at * HEAD_DIM : group * span + (at + 1) * HEAD_DIM] = head
            projected = following

        target = final if last else after_ref
        step = model // 4
        finals = []
        for at in range(0, model, step):
            cut = slice(at, at + step)
            product = jnp.dot(
                attended[...], o_ref[:, cut], preferred_element_type=jnp.float32
            )
            target[:, cut] = (state[:, cut].astype(jnp.float32) + product).astype(jnp.bfloat16)
            if last:
                copy = pltpu.make_async_copy(
                    final.at[:, cut],
                    outputs.at[jnp.clip(slot, 0, micro - 1), :, cut],
                    final_sem.at[at // step],
                )
                copy.start()
                finals.append(copy)
        for copy in finals:
            copy.wait()

    if turn > 0:

        @pl.when(wrote)
        def _():
            earlier.wait()


def take_turn(turn, last, micro, fresh, hidden, before, outputs, tables, keep, qkv, out_weight):
    rows, model = (fresh.shape[1], fresh.shape[2])
    operands, specs = [], []
    if turn < micro:
        operands.append(fresh)
        specs.append(VMEM)
    if turn > 0:
        operands += [hidden, before]
        specs += [VMEM, VMEM]
    aliases = {}
    if turn > 1:
        aliases = {len(operands): 0 if last else 1}
        operands.append(outputs)
        specs.append(ANY)
    operands += [*tables, keep, qkv, out_weight]
    specs += [VMEM] * len(tables) + [VMEM, ANY, VMEM]
    shapes, out_specs = [], []
    if not last:
        shapes.append(pltpu.VMEM((rows, model), jnp.bfloat16))
        out_specs.append(VMEM)
    if turn > 0:
        shapes.append(jax.ShapeDtypeStruct((micro, rows, model), jnp.bfloat16))
        out_specs.append(ANY)
    streams = GROUPS - RESIDENT
    results = pl.pallas_call(
        functools.partial(turn_body, turn, last, micro),
        out_shape=shapes,
        in_specs=specs,
        out_specs=out_specs,
        scratch_shapes=[
            pltpu.VMEM((rows, model), jnp.bfloat16),
            pltpu.VMEM((rows, model), jnp.bfloat16),
            pltpu.VMEM((rows, model), jnp.bfloat16),
            pltpu.VMEM((streams, model, 3 * model // GROUPS), jnp.bfloat16),
            pltpu.VMEM((rows, model) if last else (16, 128), jnp.bfloat16),
            pltpu.SemaphoreType.DMA((streams, 3)),
            pltpu.SemaphoreType.DMA,
            pltpu.SemaphoreType.DMA((4,)),
        ],
        input_output_aliases=aliases,
        compiler_params=pltpu.CompilerParams(vmem_limit_bytes=24 * MIB),
        name=f"turn_{turn}",
    )(*operands)
    after = None if last else results[0]
    outputs = results[-1] if turn > 0 else None
    return after, outputs


def body(inputs, order, image_start, image_len, norm_gain, qkv_weight, q_gain, k_gain, o_weight):
    section_count = lax.axis_size("section")
    micro = order.shape[1]
    row_count, model = inputs.shape
    rows = row_count // micro
    gathered = lax.all_gather(qkv_weight[0], "dp", axis=0, tiled=True)

    fresh = jnp.take(inputs.reshape(micro, rows, model), order[0], axis=0)
    starts = jnp.take(image_start[0], order[0])[:, None]
    ends = starts + jnp.take(image_len[0], order[0])[:, None]
    position = jnp.arange(rows, dtype=jnp.int32)
    inside = (position >= starts) & (position < ends)
    causal = position[None, :] <= position[:, None]
    allowed = (causal[None] | (inside[:, :, None] & inside[:, None, :])).astype(jnp.float32)
    gain_query = q_gain * (HEAD_DIM**-0.5 * math.log2(math.e))
    pair = jnp.arange(2 * HEAD_DIM, dtype=jnp.int32) // HEAD_DIM
    ones_pair = (pair[:, None] == pair[None, :]).astype(jnp.bfloat16)
    tables = (allowed, norm_gain, gain_query, k_gain, ones_pair)

    keep, out_weight = load_weights(gathered, o_weight[0])
    turns = micro + section_count - 1
    pairs = [(i, i + 1) for i in range(section_count - 1)]
    hidden = before = outputs = None
    for turn in range(turns):
        last = turn == turns - 1
        before, outputs = take_turn(
            turn, last, micro, fresh, hidden, before, outputs, tables, keep, gathered, out_weight
        )
        if not last:
            hidden = lax.ppermute(before, "section", pairs)
    return outputs.reshape(1, row_count, model)


def solution(mesh):
    in_specs = (
        P("dp", None),
        P("dp", None),
        P("dp", None),
        P("dp", None),
        P("section", None),
        P("section", "dp", None),
        P("section", None),
        P("section", None),
        P("section", None, None),
    )
    out_specs = P("section", "dp", None)
    return jax.shard_map(body, mesh=mesh, in_specs=in_specs, out_specs=out_specs, check_vma=False)
```

time: 545 us -> 338 us (0.62)
  waiting for transfers between devices: 416 us -> 245 us
  other arithmetic: 39.8 us -> 3.18 us
  matrix products: 35.9 us -> 0 us
  Pallas kernels: 0 us -> 28 us
  local copies, waits for them, and re-layouts: 23.8 us -> 30.4 us
    ppermute x9 -> x8, waiting for transfers between devices: 321 us -> 150 us  [body(): hidden = lax.ppermute(before, 'section', pairs)]
    dot_general x8 -> x0, matrix products: 35.9 us -> none  [the longest x2 20.3 us: project(): jnp.dot(normalize(state, gain), gathered, preferred_element_type=jnp.floa...]
    select_n x23 -> x5, other arithmetic: 30.7 us -> 2.15 us  [the longest x3 1.49 us: body(): fresh = jnp.take(inputs.reshape(micro, rows, model), order[0], axis=0)]
    pallas_call x0 -> x10, Pallas kernels: none -> 28 us  [the longest x9 25.3 us: take_turn(): pl.pallas_call(functools.partial(turn_body, turn, last, micro), out_shape...]
    unnamed x2 -> x42, local copies, waits for them, and re-layouts: 0.01 us -> 27.2 us
    cond x22 -> x0, local copies, waits for them, and re-layouts: 14.4 us -> none
    ppermute x9 -> x8, starting transfers between devices: 11.6 us -> 11.7 us  [body(): hidden = lax.ppermute(before, 'section', pairs)]
  transfers between devices with their start and end apart: 10 -> 9, of which waited for: 10 -> 9; matrix products, arithmetic and copies ran while one was open for 4% -> 2% of each run, Pallas kernels for 0% -> 0%
where the time goes in v1:
time: 338 us; the launch traced here: 332 us
  waiting for transfers between devices  245 us (72%)
  local copies, waits for them, and re-layouts  30.4 us (9%)
  Pallas kernels  28 us (8%)
  between operations  13.9 us (4%)
  starting transfers between devices  11.7 us (3%)
    ppermute x8, waiting for transfers between devices, body(): hidden = lax.ppermute(before, 'section', pairs)  150 us
    all_gather x1, waiting for transfers between devices, body(): gathered = lax.all_gather(qkv_weight[0], 'dp', axis=0, tiled=True)  93.8 us
    unnamed x42, local copies, waits for them, and re-layouts  27.2 us
    pallas_call x9, Pallas kernels, take_turn(): pl.pallas_call(functools.partial(turn_body, turn, last, micro), out_shape...  25.3 us
    ppermute x8, starting transfers between devices, body(): hidden = lax.ppermute(before, 'section', pairs)  11.7 us
  transfers between devices with their start and end apart: 9, of which 9 were waited for; matrix products, arithmetic and copies ran while one was open for 2% of the time, Pallas kernels for 0%

profile of v1, /device:TPU:224, one launch (start us, length us, event | category | flops | bytes accessed | tf_op | source)
XLA Modules:
  0.0 331.8 jit_solution(5218420077877596285)
XLA Ops:
  6.5 0.0 copy-start
  6.5 0.0 all-gather.3.cloned.1.call-start
  6.5 0.7 all-gather.3.cloned.1.call-update
  7.3 0.7 compare_select_fusion.1
  7.9 1.3 gather_fusion.1
  9.2 1.3 gather_fusion.2
  10.5 0.7 fusion
  11.2 0.0 copy-done
  11.2 0.6 gather_fusion
  11.8 0.7 broadcast_select_fusion.1
  12.5 0.1 compare_and_fusion
  12.6 0.1 compare_convert_fusion.refs_5_.refs_7_
  12.7 0.1 or_convert_fusion.refs_1_.refs_3_
  12.8 0.7 broadcast_multiply_fusion.refs_3_.refs_5_
  13.5 0.2 broadcast_select_fusion.refs_0_
  13.7 93.8 %all-gather.3.cloned.1.call-done = bf16[1,2048,6144]{2,1,0:T(8,128)(2,1)} async-done(((bf16[1,64,6144]{2,1,0:T(8,128)(2,1)}), bf16[1,2048,6144]{2,1,0:T(8,128)(2,1)}) %all-gather.3.cloned.1.call-update) | async-done | bytes 25165840 | tf_op jit(solution)/shard_map/all_gather | solution.py:261
  107.5 8.2 %copy-done.2 = bf16[1,2048,6144]{2,1,0:T(8,128)(2,1)S(1)} copy-done((bf16[1,2048,6144]{2,1,0:T(8,128)(2,1)S(1)}, bf16[1,2048,6144]{2,1,0:T(8,128)(2,1)}, u32[]{:S(2)}) %copy-start.2) | copy-done | bytes 25165848
  115.7 3.4 %copy-done.8 = bf16[1,2048,2048]{2,1,0:T(8,128)(2,1)S(1)} copy-done((bf16[1,2048,2048]{2,1,0:T(8,128)(2,1)S(1)}, bf16[1,2048,2048]{2,1,0:T(8,128)(2,1)}, u32[]{:S(2)}) %copy-start.8) | copy-done | bytes 8388632
  119.0 2.6 load_weights.1
  121.7 0.0 copy-start.3
  121.7 4.6 %copy-done.3 = bf16[2,2048,1536]{2,1,0:T(8,128)(2,1)} copy-done((bf16[2,2048,1536]{2,1,0:T(8,128)(2,1)}, bf16[2,2048,1536]{2,1,0:T(8,128)(2,1)S(1)}, u32[]{:S(2)}) %copy-start.3) | copy-done | bytes 12582936
  126.3 0.0 copy-done.9
  126.3 0.0 copy-done.10
  126.3 7.6 %copy-done.4 = bf16[2,2048,1536]{2,1,0:T(8,128)(2,1)S(1)} copy-done((bf16[2,2048,1536]{2,1,0:T(8,128)(2,1)S(1)}, bf16[2,2048,1536]{2,1,0:T(8,128)(2,1)}, u32[]{:S(2)}) %copy-start.4) | copy-done | bytes 12582936
  133.9 0.1 turn_0.1.refs_2_
  134.0 1.3 collective-permute-start
  135.3 14.7 %collective-permute-done.refs_1_ = bf16[128,2048]{1,0:T(8,128)(2,1)S(1)} collective-permute-done((bf16[128,2048]{1,0:T(8,128)(2,1)S(1)}, bf16[128,2048]{1,0:T(8,128)(2,1)S(1)}, u32[]{:S(2)}, u32[]{:S(2)}) %collective-permute-start) | collective-permute-done | bytes 524320 | tf_op jit(solution)/shard_map/ppermute | solution.py:285
  150.0 0.0 copy-done.5
  150.0 5.5 %turn_1.1 = (bf16[128,2048]{1,0:T(8,128)(2,1)S(1)}, bf16[2,128,2048]{2,1,0:T(8,128)(2,1)}) custom-call(bf16[2,128,2048]{2,1,0:T(8,128)(2,1)S(1)} %broadcast_select_fusion.refs_0_, bf16[128,2048]{1,0:T(8,128)(2,1)S(1)} %collective-permute-done.refs_1_, bf16[128,2048]{1,0:T(8,128)(2,1)S(1)} %turn_0.1.refs_2_, ...), custom_call_target="tpu_custom_call" | custom-call | tf_op jit(solution)/shard_map/turn_1/pallas_call | solution.py:232
  155.5 1.3 collective-permute-start.1
  156.8 13.9 %collective-permute-done.1.refs_0_ = bf16[128,2048]{1,0:T(8,128)(2,1)S(1)} collective-permute-done((bf16[128,2048]{1,0:T(8,128)(2,1)S(1)}, bf16[128,2048]{1,0:T(8,128)(2,1)S(1)}, u32[]{:S(2)}, u32[]{:S(2)}) %collective-permute-start.1) | collective-permute-done | bytes 524320 | tf_op jit(solution)/shard_map/ppermute | solution.py:285
  170.7 3.4 %copy-done.6 = bf16[2048,2048]{1,0:T(8,128)(2,1)S(1)} copy-done((bf16[2048,2048]{1,0:T(8,128)(2,1)S(1)}, bf16[2048,2048]{1,0:T(8,128)(2,1)}, u32[]{:S(2)}) %copy-start.6) | copy-done | bytes 8388632
  174.1 0.1 turn_2.1
  174.2 0.0 slice-start.1
  174.2 1.6 collective-permute-start.2
  175.8 13.1 %collective-permute-done.2.refs_0_ = bf16[128,2048]{1,0:T(8,128)(2,1)S(1)} collective-permute-done((bf16[128,2048]{1,0:T(8,128)(2,1)S(1)}, bf16[128,2048]{1,0:T(8,128)(2,1)S(1)}, u32[]{:S(2)}, u32[]{:S(2)}) %collective-permute-start.2) | collective-permute-done | bytes 524320 | tf_op jit(solution)/shard_map/ppermute | solution.py:285
  188.8 0.0 copy-done.7
  188.8 0.3 turn_3.1
  189.1 1.6 collective-permute-start.3
  190.7 13.1 %collective-permute-done.3.refs_0_ = bf16[128,2048]{1,0:T(8,128)(2,1)S(1)} collective-permute-done((bf16[128,2048]{1,0:T(8,128)(2,1)S(1)}, bf16[128,2048]{1,0:T(8,128)(2,1)S(1)}, u32[]{:S(2)}, u32[]{:S(2)}) %collective-permute-start.3) | collective-permute-done | bytes 524320 | tf_op jit(solution)/shard_map/ppermute | solution.py:285
  203.8 0.0 slice-done
  203.8 0.0 slice-done.1
  203.8 0.0 slice-start.4
  203.8 0.4 turn_4.1
  204.2 1.6 collective-permute-start.4
  205.7 12.4 %collective-permute-done.4.refs_0_ = bf16[128,2048]{1,0:T(8,128)(2,1)S(1)} collective-permute-done((bf16[128,2048]{1,0:T(8,128)(2,1)S(1)}, bf16[128,2048]{1,0:T(8,128)(2,1)S(1)}, u32[]{:S(2)}, u32[]{:S(2)}) %collective-permute-start.4) | collective-permute-done | bytes 524320 | tf_op jit(solution)/shard_map/ppermute | solution.py:285
  218.1 0.0 slice-done.2
  218.1 0.0 slice-done.3
  218.1 0.0 slice-start.6
  218.1 0.4 turn_5.1
  218.5 1.6 collective-permute-start.5
  220.1 11.4 %collective-permute-done.5.refs_0_ = bf16[128,2048]{1,0:T(8,128)(2,1)S(1)} collective-permute-done((bf16[128,2048]{1,0:T(8,128)(2,1)S(1)}, bf16[128,2048]{1,0:T(8,128)(2,1)S(1)}, u32[]{:S(2)}, u32[]{:S(2)}) %collective-permute-start.5) | collective-permute-done | bytes 524320 | tf_op jit(solution)/shard_map/ppermute | solution.py:285
  231.5 0.0 slice-done.4
  231.5 0.0 slice-done.5
  231.5 0.0 slice-start.8
  231.5 0.6 turn_6.1
  232.2 1.6 collective-permute-start.6
  233.7 60.8 %collective-permute-done.6.refs_0_ = bf16[128,2048]{1,0:T(8,128)(2,1)S(1)} collective-permute-done((bf16[128,2048]{1,0:T(8,128)(2,1)S(1)}, bf16[128,2048]{1,0:T(8,128)(2,1)S(1)}, u32[]{:S(2)}, u32[]{:S(2)}) %collective-permute-start.6) | collective-permute-done | bytes 524320 | tf_op jit(solution)/shard_map/ppermute | solution.py:285
  294.5 0.0 slice-done.6
  294.5 8.5 %turn_7.1 = (bf16[128,2048]{1,0:T(8,128)(2,1)S(1)}, bf16[2,128,2048]{2,1,0:T(8,128)(2,1)}) custom-call(bf16[128,2048]{1,0:T(8,128)(2,1)S(1)} %collective-permute-done.6.refs_0_, bf16[128,2048]{1,0:T(8,128)(2,1)S(1)} %get-tuple-element.34.refs_1_, bf16[2,128,2048]{2,1,0:T(8,128)(2,1)} %get-tuple-element.35.refs_2_, ...), custom_call_target="tpu_custom_call", output_to_operand_aliasing={{1}: (2, {})} | custom-call | tf_op jit(solution)/shard_map/turn_7/pallas_call | solution.py:232
  303.1 1.3 collective-permute-start.7
  304.4 10.9 %collective-permute-done.7.refs_0_ = bf16[128,2048]{1,0:T(8,128)(2,1)S(1)} collective-permute-done((bf16[128,2048]{1,0:T(8,128)(2,1)S(1)}, bf16[128,2048]{1,0:T(8,128)(2,1)S(1)}, u32[]{:S(2)}, u32[]{:S(2)}) %collective-permute-start.7) | collective-permute-done | bytes 524320 | tf_op jit(solution)/shard_map/ppermute | solution.py:285
  315.3 9.4 %turn_8.1 = bf16[2,128,2048]{2,1,0:T(8,128)(2,1)} custom-call(bf16[128,2048]{1,0:T(8,128)(2,1)S(1)} %collective-permute-done.7.refs_0_, bf16[128,2048]{1,0:T(8,128)(2,1)S(1)} %get-tuple-element.36.refs_1_, bf16[2,128,2048]{2,1,0:T(8,128)(2,1)} %get-tuple-element.37.refs_2_, ...), custom_call_target="tpu_custom_call", output_to_operand_aliasing={{}: (2, {})} | custom-call | tf_op jit(solution)/shard_map/turn_8/pallas_call | solution.py:232
  324.7 0.0 copy-done.1
  (28 shorter events, 0.1 us)
Async XLA Ops:
  6.5 4.6 %copy-start = (bf16[256,2048]{1,0:T(8,128)(2,1)S(1)}, bf16[256,2048]{1,0:T(8,128)(2,1)}, u32[]{:S(2)}) copy-start(bf16[256,2048]{1,0:T(8,128)(2,1)} %param.11) | copy-start | bytes 3145732
  6.5 101.0 %all-gather.3.cloned.1.call-start = ((), (), s32[]{:S(2)}) async-start(), calls=%async_computation | async-start | bytes 25952256 | tf_op jit(solution)/shard_map/all_gather | solution.py:261
  107.5 8.2 %copy-start.2 = (bf16[1,2048,6144]{2,1,0:T(8,128)(2,1)S(1)}, bf16[1,2048,6144]{2,1,0:T(8,128)(2,1)}, u32[]{:S(2)}) copy-start(bf16[1,2048,6144]{2,1,0:T(8,128)(2,1)} %all-gather.3.cloned.1.call-done) | copy-start | bytes 75497472
  115.7 3.4 %copy-start.8 = (bf16[1,2048,2048]{2,1,0:T(8,128)(2,1)S(1)}, bf16[1,2048,2048]{2,1,0:T(8,128)(2,1)}, u32[]{:S(2)}) copy-start(bf16[1,2048,2048]{2,1,0:T(8,128)(2,1)} %param.19) | copy-start | bytes 25165828
  119.0 7.3 %copy-start.9 = (f32[1,2048]{1,0:T(1,128)S(1)}, f32[1,2048]{1,0:T(1,128)}, u32[]{:S(2)}) copy-start(f32[1,2048]{1,0:T(1,128)} %refs_4_.17) | copy-start | bytes 24580
  119.0 7.3 %copy-start.10 = (f32[1,2048]{1,0:T(1,128)S(1)}, f32[1,2048]{1,0:T(1,128)}, u32[]{:S(2)}) copy-start(f32[1,2048]{1,0:T(1,128)} %refs_6_.15) | copy-start | bytes 24580
  121.7 4.6 %copy-start.3 = (bf16[2,2048,1536]{2,1,0:T(8,128)(2,1)}, bf16[2,2048,1536]{2,1,0:T(8,128)(2,1)S(1)}, u32[]{:S(2)}) copy-start(bf16[2,2048,1536]{2,1,0:T(8,128)(2,1)S(1)} %get-tuple-element.22.refs_6_.refs_8_) | copy-start | bytes 37748740
  126.3 23.7 %copy-start.5 = (bf16[2048,2048]{1,0:T(8,128)(2,1)}, bf16[2048,2048]{1,0:T(8,128)(2,1)S(1)}, u32[]{:S(2)}) copy-start(bf16[2048,2048]{1,0:T(8,128)(2,1)S(1)} %get-tuple-element.23.refs_8_.refs_10_) | copy-start | bytes 25165828
  126.3 7.6 %copy-start.4 = (bf16[2,2048,1536]{2,1,0:T(8,128)(2,1)S(1)}, bf16[2,2048,1536]{2,1,0:T(8,128)(2,1)}, u32[]{:S(2)}) copy-start(bf16[2,2048,1536]{2,1,0:T(8,128)(2,1)} %copy-done.3) | copy-start | bytes 37748740
  134.0 16.0 %collective-permute-start = (bf16[128,2048]{1,0:T(8,128)(2,1)S(1)}, bf16[128,2048]{1,0:T(8,128)(2,1)S(1)}, u32[]{:S(2)}, u32[]{:S(2)}) collective-permute-start(bf16[128,2048]{1,0:T(8,128)(2,1)S(1)} %turn_0.1.refs_2_), channel_id=1, source_target_pairs={{0,32},{32,64},{64,96},{96,128},{128,160},{160,192},{192,224},{1,3... | collective-permute-start | bytes 1572872 | tf_op jit(solution)/shard_map/ppermute | solution.py:285
  155.5 15.2 %collective-permute-start.1 = (bf16[128,2048]{1,0:T(8,128)(2,1)S(1)}, bf16[128,2048]{1,0:T(8,128)(2,1)S(1)}, u32[]{:S(2)}, u32[]{:S(2)}) collective-permute-start(bf16[128,2048]{1,0:T(8,128)(2,1)S(1)} %get-tuple-element.24.refs_1_), channel_id=1, source_target_pairs={{0,32},{32,64},{64,96},{96,128},{128,160},{160,192},{192,224},{1,3... | collective-permute-start | bytes 1572872 | tf_op jit(solution)/shard_map/ppermute | solution.py:285
  170.7 3.4 %copy-start.6 = (bf16[2048,2048]{1,0:T(8,128)(2,1)S(1)}, bf16[2048,2048]{1,0:T(8,128)(2,1)}, u32[]{:S(2)}) copy-start(bf16[2048,2048]{1,0:T(8,128)(2,1)} %copy-done.5) | copy-start | bytes 25165828
  174.1 14.8 %copy-start.7 = (bf16[2048,2048]{1,0:T(8,128)(2,1)S(1)}, bf16[2048,2048]{1,0:T(8,128)(2,1)}, u32[]{:S(2)}) copy-start(bf16[2048,2048]{1,0:T(8,128)(2,1)} %copy-done.5) | copy-start | bytes 25165828
  174.1 29.7 %slice-start = ((s8[8388608]{0:T(1024)(128)(4,1)}), s8[4194304]{0:T(1024)(128)(4,1)S(1)}, s32[]{:S(2)}) async-start(s8[8388608]{0:T(1024)(128)(4,1)} %bitcast.26), calls=%async_computation.1 | async-start | bytes 8388608
  174.2 29.6 %slice-start.1 = ((s8[8388608]{0:T(1024)(128)(4,1)}), s8[4194304]{0:T(1024)(128)(4,1)S(1)}, s32[]{:S(2)}) async-start(s8[8388608]{0:T(1024)(128)(4,1)} %bitcast.26), calls=%async_computation.2 | async-start | bytes 8388608
  174.2 14.6 %collective-permute-start.2 = (bf16[128,2048]{1,0:T(8,128)(2,1)S(1)}, bf16[128,2048]{1,0:T(8,128)(2,1)S(1)}, u32[]{:S(2)}, u32[]{:S(2)}) collective-permute-start(bf16[128,2048]{1,0:T(8,128)(2,1)S(1)} %get-tuple-element.26.refs_1_), channel_id=1, source_target_pairs={{0,32},{32,64},{64,96},{96,128},{128,160},{160,192},{192,224},{1,3... | collective-permute-start | bytes 1572872 | tf_op jit(solution)/shard_map/ppermute | solution.py:285
  188.8 29.3 %slice-start.2 = ((s8[8388608]{0:T(1024)(128)(4,1)}), s8[4194304]{0:T(1024)(128)(4,1)S(1)}, s32[]{:S(2)}) async-start(s8[8388608]{0:T(1024)(128)(4,1)} %bitcast.28), calls=%async_computation.3 | async-start | bytes 8388608
  189.1 14.6 %collective-permute-start.3 = (bf16[128,2048]{1,0:T(8,128)(2,1)S(1)}, bf16[128,2048]{1,0:T(8,128)(2,1)S(1)}, u32[]{:S(2)}, u32[]{:S(2)}) collective-permute-start(bf16[128,2048]{1,0:T(8,128)(2,1)S(1)} %get-tuple-element.28.refs_1_), channel_id=1, source_target_pairs={{0,32},{32,64},{64,96},{96,128},{128,160},{160,192},{192,224},{1,3... | collective-permute-start | bytes 1572872 | tf_op jit(solution)/shard_map/ppermute | solution.py:285
  203.8 14.3 %slice-start.3 = ((s8[8388608]{0:T(1024)(128)(4,1)}), s8[4194304]{0:T(1024)(128)(4,1)S(1)}, s32[]{:S(2)}) async-start(s8[8388608]{0:T(1024)(128)(4,1)} %bitcast.28), calls=%async_computation.4 | async-start | bytes 8388608
  203.8 27.7 %slice-start.4 = ((s8[8388608]{0:T(1024)(128)(4,1)}), s8[4194304]{0:T(1024)(128)(4,1)S(1)}, s32[]{:S(2)}) async-start(s8[8388608]{0:T(1024)(128)(4,1)} %bitcast.30), calls=%async_computation.5 | async-start | bytes 8388608
  204.2 13.9 %collective-permute-start.4 = (bf16[128,2048]{1,0:T(8,128)(2,1)S(1)}, bf16[128,2048]{1,0:T(8,128)(2,1)S(1)}, u32[]{:S(2)}, u32[]{:S(2)}) collective-permute-start(bf16[128,2048]{1,0:T(8,128)(2,1)S(1)} %get-tuple-element.30.refs_1_), channel_id=1, source_target_pairs={{0,32},{32,64},{64,96},{96,128},{128,160},{160,192},{192,224},{1,3... | collective-permute-start | bytes 1572872 | tf_op jit(solution)/shard_map/ppermute | solution.py:285
  218.1 13.4 %slice-start.5 = ((s8[8388608]{0:T(1024)(128)(4,1)}), s8[4194304]{0:T(1024)(128)(4,1)S(1)}, s32[]{:S(2)}) async-start(s8[8388608]{0:T(1024)(128)(4,1)} %bitcast.30), calls=%async_computation.6 | async-start | bytes 8388608
  218.1 76.4 %slice-start.6 = ((s8[8388608]{0:T(1024)(128)(4,1)}), s8[4194304]{0:T(1024)(128)(4,1)S(1)}, s32[]{:S(2)}) async-start(s8[8388608]{0:T(1024)(128)(4,1)} %bitcast.32), calls=%async_computation.7 | async-start | bytes 8388608
  218.5 13.0 %collective-permute-start.5 = (bf16[128,2048]{1,0:T(8,128)(2,1)S(1)}, bf16[128,2048]{1,0:T(8,128)(2,1)S(1)}, u32[]{:S(2)}, u32[]{:S(2)}) collective-permute-start(bf16[128,2048]{1,0:T(8,128)(2,1)S(1)} %get-tuple-element.32.refs_1_), channel_id=1, source_target_pairs={{0,32},{32,64},{64,96},{96,128},{128,160},{160,192},{192,224},{1,3... | collective-permute-start | bytes 1572872 | tf_op jit(solution)/shard_map/ppermute | solution.py:285
  231.5 63.0 %slice-start.7 = ((s8[8388608]{0:T(1024)(128)(4,1)}), s8[4194304]{0:T(1024)(128)(4,1)S(1)}, s32[]{:S(2)}) async-start(s8[8388608]{0:T(1024)(128)(4,1)} %bitcast.32), calls=%async_computation.8 | async-start | bytes 8388608
  231.5 83.8 %slice-start.8 = ((s8[8388608]{0:T(1024)(128)(4,1)}), s8[4194304]{0:T(1024)(128)(4,1)S(1)}, s32[]{:S(2)}) async-start(s8[8388608]{0:T(1024)(128)(4,1)} %bitcast.34), calls=%async_computation.9 | async-start | bytes 8388608
  232.2 62.4 %collective-permute-start.6 = (bf16[128,2048]{1,0:T(8,128)(2,1)S(1)}, bf16[128,2048]{1,0:T(8,128)(2,1)S(1)}, u32[]{:S(2)}, u32[]{:S(2)}) collective-permute-start(bf16[128,2048]{1,0:T(8,128)(2,1)S(1)} %get-tuple-element.34.refs_1_), channel_id=1, source_target_pairs={{0,32},{32,64},{64,96},{96,128},{128,160},{160,192},{192,224},{1,3... | collective-permute-start | bytes 1572872 | tf_op jit(solution)/shard_map/ppermute | solution.py:285
  294.5 20.8 %slice-start.9 = ((s8[8388608]{0:T(1024)(128)(4,1)}), s8[4194304]{0:T(1024)(128)(4,1)S(1)}, s32[]{:S(2)}) async-start(s8[8388608]{0:T(1024)(128)(4,1)} %bitcast.34), calls=%async_computation.10 | async-start | bytes 8388608
  303.1 12.2 %collective-permute-start.7 = (bf16[128,2048]{1,0:T(8,128)(2,1)S(1)}, bf16[128,2048]{1,0:T(8,128)(2,1)S(1)}, u32[]{:S(2)}, u32[]{:S(2)}) collective-permute-start(bf16[128,2048]{1,0:T(8,128)(2,1)S(1)} %get-tuple-element.36.refs_1_), channel_id=1, source_target_pairs={{0,32},{32,64},{64,96},{96,128},{128,160},{160,192},{192,224},{1,3... | collective-permute-start | bytes 1572872 | tf_op jit(solution)/shard_map/ppermute | solution.py:285
  315.3 9.4 %copy-start.1 = (bf16[256,2048]{1,0:T(8,128)(2,1)S(1)}, bf16[256,2048]{1,0:T(8,128)(2,1)}, u32[]{:S(2)}) copy-start(bf16[256,2048]{1,0:T(8,128)(2,1)} %param.11) | copy-start | bytes 3145732
Sparse Core Ops, SparseCore 0:
  9.9 97.5 all-gather.2
